TPU v7x, 256 devices: a whole 4x4x8 slice. The times are simulated.
256 devices in a mesh: wide: 32 (over z, y), slab: 8 (over x, core).
Axes of the slice: x: 4, y: 4, z: 8, core: 2. Of those that a mesh axis runs over, the one named last changes fastest.
Arguments:
- thermal_state: float32 [32, 128, 32, 1024], P('wide', 'slab'), may hold values from -5 to 5
- thermal_spreading_rate: bfloat16 [32, 128, 32, 1024], P('wide', 'slab'), may hold values from 0.5 to 1.5
- flow_speed_vector: bfloat16 [3, 32, 128, 32, 1024], P(None, 'wide', 'slab'), may hold values from -0.796875 to 0.796875
- interface_guess: float32 [32, 2048], P('wide', 'slab'), may hold values from -4 to 4
- partner_facing_rows: int32 [32, 2048], P('wide', 'slab'), may hold values from 0 to 2047, each once within a row
- mismatch_change_matrix: float32 [32, 2048, 128], P('wide', 'slab'), may hold values from -5 to 5
- output_change_matrix: float32 [32, 2048, 128], P('wide', 'slab'), may hold values from -1.8 to 1.8
Outputs:
- temperature_out: float32 [32, 128, 32, 1024], P('wide', 'slab')
- updated_interface_guess: float32 [32, 2048], P('wide', 'slab')
- unitary_basis_factor: float32 [32, 2048, 128], P('wide', 'slab')
Inputs may be any that keep to these rules, and one draw needn't show every extreme that they name: `partner_facing_rows`: each partition's rows of matching are a permutation of its partner's interface rows.
All inputs are finite; a program needn't handle non-finite values.
Results may differ from a plain program's by a relative error of at most 0.0003.
Values may be sent and summed in bfloat16 or wider, within the bound.
No kernel may reach another device: no remote copies, remote signals or barrier semaphores. Data moves between devices by JAX's collectives and lax.ppermute only.
A program may use at most 64 MiB of HBM per device.

v0:
```python
import math
import jax
import jax.numpy as jnp
from jax import lax
from jax.sharding import PartitionSpec as P

INTERFACE_STRIP = 64
SWEEPS = 4
STEP_SIZE = 0.11


def padded(cells, sides, width):
    for axis, dim in sides:
        count = lax.axis_size(axis)
        ends = count - 1
        head = lax.slice_in_dim(cells, 0, width, axis=dim)
        tail = lax.slice_in_dim(cells, cells.shape[dim] - width, cells.shape[dim], axis=dim)
        cells = jnp.concatenate(
            [
                lax.ppermute(tail, axis, [(i, (i + 1) % count) for i in range(ends)]),
                cells,
                lax.ppermute(head, axis, [((i + 1) % count, i) for i in range(ends)]),
            ],
            axis=dim,
        )
    return cells


def partner(value, axis, stride):
    mask = 2**stride
    pairs = [(source, source ^ mask) for source in range(lax.axis_size(axis))]
    return lax.ppermute(value, axis, pairs)


def surround_wrapper(block_rows, mirror_layer):
    bottom = jnp.zeros((block_rows.shape[0], 1, block_rows.shape[2]), block_rows.dtype)
    stacked = jnp.concatenate([bottom, block_rows, mirror_layer[:, None, :]], axis=1)
    return jnp.pad(stacked, ((0, 0), (0, 0), (1, 1)))


def march_forward(bordered_array, diffuse_subdomain, subdomain_flow_speed):
    centre = bordered_array[1:-1, 1:-1, 1:-1]
    plus_first = bordered_array[2:, 1:-1, 1:-1]
    minus_first = bordered_array[:-2, 1:-1, 1:-1]
    plus_second = bordered_array[1:-1, 2:, 1:-1]
    minus_second = bordered_array[1:-1, :-2, 1:-1]
    plus_third = bordered_array[1:-1, 1:-1, 2:]
    minus_third = bordered_array[1:-1, 1:-1, :-2]
    spread = (
        plus_first
        + minus_first
        + plus_second
        + minus_second
        + plus_third
        + minus_third
        - 6.0 * centre
    )
    carried = 0.5 * (
        subdomain_flow_speed[0].astype(jnp.float32) * (plus_first - minus_first)
        + subdomain_flow_speed[1].astype(jnp.float32) * (plus_second - minus_second)
        + subdomain_flow_speed[2].astype(jnp.float32) * (plus_third - minus_third)
    )
    return centre + STEP_SIZE * (diffuse_subdomain.astype(jnp.float32) * spread - carried)


def shards(
    thermal_state,
    thermal_spreading_rate,
    flow_speed_vector,
    interface_guess,
    partner_facing_rows,
    mismatch_change_matrix,
    output_change_matrix,
):
    subdomain_thermal_state = thermal_state[0]
    diffuse_subdomain = thermal_spreading_rate[0]
    subdomain_flow_speed = flow_speed_vector[:, 0]
    layer_stack = subdomain_thermal_state.shape[0]
    vertical_extent = subdomain_thermal_state.shape[1]
    rows_dev = interface_guess.shape[1]
    mirror_layer = jnp.repeat(interface_guess[0].reshape(layer_stack, -1), INTERFACE_STRIP, axis=1)
    panel = mismatch_change_matrix[0]
    gram_local = lax.dot_general(
        panel,
        panel,
        (((0,), (0,)), ((), ())),
        precision=lax.Precision.HIGHEST,
        preferred_element_type=jnp.float32,
    )
    ghost_padded = jnp.pad(mirror_layer, ((1, 1), (0, 0)))
    for sweep in range(SWEEPS):
        widened_array = padded(subdomain_thermal_state, (("slab", 0),), 1)
        subdomain_thermal_state = march_forward(
            surround_wrapper(widened_array, ghost_padded), diffuse_subdomain, subdomain_flow_speed
        )
    face_means = jnp.mean(
        subdomain_thermal_state[:, vertical_extent - 1, :].reshape(
            layer_stack, -1, INTERFACE_STRIP
        ),
        axis=2,
    )
    face_means = face_means.reshape(1, rows_dev)
    top_bit = lax.axis_size("wide").bit_length() - 2
    partner_own = partner(face_means, "wide", top_bit)
    partner_all = lax.all_gather(partner_own, "slab", axis=1, tiled=True)
    tilde = jnp.take(partner_all[0], partner_facing_rows[0], axis=0)
    resid = tilde - interface_guess[0]
    proj_local = jnp.dot(
        resid, panel, precision=lax.Precision.HIGHEST, preferred_element_type=jnp.float32
    )
    gram_matrix, projection = lax.psum((gram_local, proj_local), ("wide", "slab"))
    lower_factor = jnp.linalg.cholesky(gram_matrix)
    half_solve = lax.linalg.triangular_solve(
        lower_factor, projection[:, None], left_side=True, lower=True
    )
    coefficients = -lax.linalg.triangular_solve(
        lower_factor, half_solve, left_side=True, lower=True, transpose_a=True
    )[:, 0]
    update = jnp.dot(
        output_change_matrix[0],
        coefficients,
        precision=lax.Precision.HIGHEST,
        preferred_element_type=jnp.float32,
    )
    updated_interface_guess = tilde + update
    total_rows = rows_dev * lax.axis_size("slab") * lax.axis_size("wide")
    scaled = lax.linalg.triangular_solve(
        lower_factor, panel, left_side=False, lower=True, transpose_a=True
    )
    unitary_basis_factor = math.sqrt(total_rows) * scaled
    return (
        subdomain_thermal_state[None],
        updated_interface_guess[None],
        unitary_basis_factor[None],
    )


def solution(mesh):
    return jax.shard_map(
        shards,
        mesh=mesh,
        in_specs=(
            P("wide", "slab", None, None),
            P("wide", "slab", None, None),
            P(None, "wide", "slab", None, None),
            P("wide", "slab"),
            P("wide", "slab"),
            P("wide", "slab", None),
            P("wide", "slab", None),
        ),
        out_specs=(P("wide", "slab", None, None), P("wide", "slab"), P("wide", "slab", None)),
        check_vma=False,
    )
```

profile of v0, /device:TPU:1, one launch (start us, length us, event | category | flops | bytes accessed | tf_op | source)
XLA Modules:
  0.0 438.8 jit_solution(339822084845978649)
XLA Ops:
  8.2 5.1 %collective-permute-start = (f32[1,32,1024]{2,1,0:T(8,128)S(1)}, f32[1,32,1024]{2,1,0:T(8,128)S(1)}, u32[]{:S(2)}, u32[]{:S(2)}) collective-permute-start(f32[1,32,1024]{2,1,0:T(8,128)S(1)} %get-tuple-element.16), channel_id=1, source_target_pairs={{1,0},{2,1},{3,2},{4,3},{5,4},{6,5},{7,6},{9,8},{10,9},{11,10},{12... | collective-permute-start | bytes 393224 | tf_op jit(solution)/shard_map/ppermute | solution.py:22
  13.4 1.9 collective-permute-start.1
  17.6 1.3 reduce.11
  19.3 237.0 %all-reduce.11.cloned.1.call-done = f32[128,128]{0,1:T(8,128)} async-done(((f32[128,128]{0,1:T(8,128)}), f32[128,128]{0,1:T(8,128)}) %all-reduce.11.cloned.1.call-update) | async-done | bytes 65552 | tf_op jit(solution)/shard_map/psum | solution.py:111
  257.9 2.3 pad_maximum_fusion.3
  260.7 7.0 %fusion.2 = f32[16,32,1024]{2,1,0:T(8,128)S(1)} fusion(f32[16,32,1024]{2,1,0:T(8,128)} %bitcast.90, f32[18,34,1024]{2,1,0:T(8,128)S(1)} %pad_maximum_fusion.3, f32[1,32,1024]{2,1,0:T(8,128)S(1)} %collective-permute-done, f32[1,32,1024]{2,1,0:T(8,128)S(1)} %copy-done.11, f32[18,1,1024]{2,1,0:T(1,128)S(1)} %broadcast_in_dim.30, ...), kind=kLoop, calls=%fused_computation.35 | loop fusion | flops 18874368 | bytes 11231232 | tf_op jit(solution)/shard_map/add | solution.py:63
  267.8 1.3 copy-done.4
  269.8 1.9 collective-permute-start.2
  271.7 3.6 collective-permute-start.3
  276.0 12.5 %cholesky.16 = f32[128,128]{1,0:T(8,128)S(1)} custom-call(f32[128,128]{1,0:T(8,128)} %fusion.45), custom_call_target="Cholesky" | custom-call | tf_op jit(solution)/shard_map/jit(cholesky)/cholesky | solution.py:112
  288.6 2.3 pad_maximum_fusion.2
  291.1 4.6 %fusion.5 = f32[16,32,1024]{2,1,0:T(8,128)S(1)} fusion(f32[16,32,1024]{2,1,0:T(8,128)S(1)} %copy-done.5, f32[18,34,1024]{2,1,0:T(8,128)S(1)} %pad_maximum_fusion.2, f32[1,32,1024]{2,1,0:T(8,128)S(1)} %collective-permute-done.2, f32[1,32,1024]{2,1,0:T(8,128)} %collective-permute-done.3, f32[18,1,1024]{2,1,0:T(1,128)S(1)} %broadcast_in_dim.30, ...), kind=kLoop, calls=%fused_computation.38 | loop fusion | flops 18874368 | bytes 11231232 | tf_op jit(solution)/shard_map/add | solution.py:63
  295.8 1.9 collective-permute-start.4
  297.7 3.8 collective-permute-start.5
  304.0 5.4 %fusion.8 = f32[16,32,1024]{2,1,0:T(8,128)S(1)} fusion(f32[16,32,1024]{2,1,0:T(8,128)S(1)} %fusion.5, f32[18,34,1024]{2,1,0:T(8,128)S(1)} %pad_maximum_fusion.1, f32[1,32,1024]{2,1,0:T(8,128)S(1)} %collective-permute-done.4, f32[1,32,1024]{2,1,0:T(8,128)S(1)} %collective-permute-done.5, f32[18,1,1024]{2,1,0:T(1,128)S(1)} %broadcast_in_dim.30, ...), kind=kLoop, calls=%fused_computation.41 | loop fusion | flops 18874368 | bytes 11231232 | tf_op jit(solution)/shard_map/add | solution.py:63
  311.4 1.9 collective-permute-start.6
  313.3 4.4 collective-permute-start.7
  319.0 10.6 %custom-call.10 = f32[1,128,128]{1,2,0:T(8,128)S(1)} custom-call(f32[1,128,128]{2,1,0:T(8,128)} %fusion.41), custom_call_target="InvertDiagBlocksLowerTriangular" | custom-call | tf_op jit(solution)/shard_map/triangular_solve | solution.py:116
  329.7 2.3 pad_maximum_fusion
  332.2 4.6 %fusion.11 = f32[16,32,1024]{2,1,0:T(8,128)S(1)} fusion(f32[16,32,1024]{2,1,0:T(8,128)S(1)} %copy-done.3, f32[18,34,1024]{2,1,0:T(8,128)S(1)} %pad_maximum_fusion, f32[1,32,1024]{2,1,0:T(8,128)S(1)} %collective-permute-done.6, f32[1,32,1024]{2,1,0:T(8,128)} %collective-permute-done.7, f32[18,1,1024]{2,1,0:T(1,128)S(1)} %broadcast_in_dim.30, ...), kind=kLoop, calls=%fused_computation.44 | loop fusion | flops 18874368 | bytes 11231232 | tf_op jit(solution)/shard_map/add | solution.py:63
  340.6 4.4 %collective-permute-done.8 = f32[1,256]{1,0:T(1,128)S(1)} collective-permute-done((f32[1,256]{1,0:T(1,128)S(1)}, f32[1,256]{1,0:T(1,128)S(1)}, u32[]{:S(2)}, u32[]{:S(2)}) %collective-permute-start.8) | collective-permute-done | bytes 1056 | tf_op jit(solution)/shard_map/ppermute | solution.py:32
  345.0 10.1 %all_gather.3 = f32[1,2048]{1,0:T(1,128)S(1)} all-gather(f32[1,256]{1,0:T(1,128)S(1)} %collective-permute-done.8), channel_id=1, replica_groups=mesh['wide'=32,'slab'=8] {'slab'}, dimensions={1}, use_global_device_ids=true | all-gather | bytes 9216 | tf_op jit(solution)/shard_map/all_gather | solution.py:105
  355.1 1.7 gather_fusion
  357.0 73.7 %psum.15 = f32[128]{0:T(128)S(1)} all-reduce(f32[128]{0:T(128)S(1)} %convolution_bitcast_fusion.2), channel_id=1, replica_groups=mesh['wide'=32,'slab'=8] {'wide','slab'}, use_global_device_ids=true, to_apply=%region_4.5 | all-reduce | flops 128 | bytes 1024 | tf_op jit(solution)/shard_map/psum | solution.py:111
  (78 shorter events, 18.4 us)
Async XLA Ops:
  7.2 8.2 %copy-start = (f32[1,256,128]{2,1,0:T(8,128)S(1)}, f32[1,256,128]{2,1,0:T(8,128)}, u32[]{:S(2)}) copy-start(f32[1,256,128]{2,1,0:T(8,128)} %param.12) | copy-start | bytes 393220
  7.2 249.1 %all-reduce.11.cloned.1.call-start = ((), (), s32[]{:S(2)}) async-start(), calls=%async_computation | async-start | bytes 131072 | tf_op jit(solution)/shard_map/psum | solution.py:111
  8.2 249.0 %collective-permute-start = (f32[1,32,1024]{2,1,0:T(8,128)S(1)}, f32[1,32,1024]{2,1,0:T(8,128)S(1)}, u32[]{:S(2)}, u32[]{:S(2)}) collective-permute-start(f32[1,32,1024]{2,1,0:T(8,128)S(1)} %get-tuple-element.16), channel_id=1, source_target_pairs={{1,0},{2,1},{3,2},{4,3},{5,4},{6,5},{7,6},{9,8},{10,9},{11,10},{12... | collective-permute-start | bytes 393224 | tf_op jit(solution)/shard_map/ppermute | solution.py:22
  13.4 243.8 %collective-permute-start.1 = (f32[1,32,1024]{2,1,0:T(8,128)S(1)}, f32[1,32,1024]{2,1,0:T(8,128)S(1)}, u32[]{:S(2)}, u32[]{:S(2)}) collective-permute-start(f32[1,32,1024]{2,1,0:T(8,128)S(1)} %get-tuple-element.15), channel_id=1, source_target_pairs={{0,1},{1,2},{2,3},{3,4},{4,5},{5,6},{6,7},{8,9},{9,10},{10,11},{11... | collective-permute-start | bytes 393224 | tf_op jit(solution)/shard_map/ppermute | solution.py:20
  257.9 2.6 copy-start.1
  257.9 2.8 copy-start.6
  257.9 2.8 copy-start.11
  260.7 14.6 %copy-start.12 = (f32[128,128]{0,1:T(8,128)S(1)}, f32[128,128]{0,1:T(8,128)}, u32[]{:S(2)}) copy-start(f32[128,128]{0,1:T(8,128)} %all-reduce.11.cloned.1.call-done) | copy-start | bytes 196612
  269.8 18.8 %collective-permute-start.2 = (f32[1,32,1024]{2,1,0:T(8,128)}, f32[1,32,1024]{2,1,0:T(8,128)S(1)}, u32[]{:S(2)}, u32[]{:S(2)}) collective-permute-start(f32[1,32,1024]{2,1,0:T(8,128)} %get-tuple-element.14), channel_id=1, source_target_pairs={{1,0},{2,1},{3,2},{4,3},{5,4},{6,5},{7,6},{9,8},{10,9},{11,10},{12... | collective-permute-start | bytes 393224 | tf_op jit(solution)/shard_map/ppermute | solution.py:22
  271.7 16.9 %collective-permute-start.3 = (f32[1,32,1024]{2,1,0:T(8,128)}, f32[1,32,1024]{2,1,0:T(8,128)}, u32[]{:S(2)}, u32[]{:S(2)}) collective-permute-start(f32[1,32,1024]{2,1,0:T(8,128)} %get-tuple-element.13), channel_id=1, source_target_pairs={{0,1},{1,2},{2,3},{3,4},{4,5},{5,6},{6,7},{8,9},{9,10},{10,11},{11... | collective-permute-start | bytes 393224 | tf_op jit(solution)/shard_map/ppermute | solution.py:20
  288.6 13.0 %copy-start.13 = (f32[128,128]{1,0:T(8,128)}, f32[128,128]{1,0:T(8,128)S(1)}, u32[]{:S(2)}) copy-start(f32[128,128]{1,0:T(8,128)S(1)} %cholesky.16) | copy-start | bytes 196612
  288.6 2.3 copy-start.5
  288.6 2.5 copy-start.7
  295.8 6.4 %collective-permute-start.4 = (f32[1,32,1024]{2,1,0:T(8,128)S(1)}, f32[1,32,1024]{2,1,0:T(8,128)S(1)}, u32[]{:S(2)}, u32[]{:S(2)}) collective-permute-start(f32[1,32,1024]{2,1,0:T(8,128)S(1)} %get-tuple-element.12), channel_id=1, source_target_pairs={{1,0},{2,1},{3,2},{4,3},{5,4},{6,5},{7,6},{9,8},{10,9},{11,10},{12... | collective-permute-start | bytes 393224 | tf_op jit(solution)/shard_map/ppermute | solution.py:22
  297.7 5.6 %collective-permute-start.5 = (f32[1,32,1024]{2,1,0:T(8,128)S(1)}, f32[1,32,1024]{2,1,0:T(8,128)S(1)}, u32[]{:S(2)}, u32[]{:S(2)}) collective-permute-start(f32[1,32,1024]{2,1,0:T(8,128)S(1)} %get-tuple-element.11), channel_id=1, source_target_pairs={{0,1},{1,2},{2,3},{3,4},{4,5},{5,6},{6,7},{8,9},{9,10},{10,11},{11... | collective-permute-start | bytes 393224 | tf_op jit(solution)/shard_map/ppermute | solution.py:20
  304.0 13.7 %copy-start.14 = (f32[128,128]{1,0:T(8,128)S(1)}, f32[128,128]{1,0:T(8,128)}, u32[]{:S(2)}) copy-start(f32[128,128]{1,0:T(8,128)} %copy-done.13) | copy-start | bytes 196612
  311.4 18.2 %collective-permute-start.6 = (f32[1,32,1024]{2,1,0:T(8,128)}, f32[1,32,1024]{2,1,0:T(8,128)S(1)}, u32[]{:S(2)}, u32[]{:S(2)}) collective-permute-start(f32[1,32,1024]{2,1,0:T(8,128)} %get-tuple-element.10), channel_id=1, source_target_pairs={{1,0},{2,1},{3,2},{4,3},{5,4},{6,5},{7,6},{9,8},{10,9},{11,10},{12... | collective-permute-start | bytes 393224 | tf_op jit(solution)/shard_map/ppermute | solution.py:22
  313.3 16.3 %collective-permute-start.7 = (f32[1,32,1024]{2,1,0:T(8,128)}, f32[1,32,1024]{2,1,0:T(8,128)}, u32[]{:S(2)}, u32[]{:S(2)}) collective-permute-start(f32[1,32,1024]{2,1,0:T(8,128)} %get-tuple-element.9), channel_id=1, source_target_pairs={{0,1},{1,2},{2,3},{3,4},{4,5},{5,6},{6,7},{8,9},{9,10},{10,11},{11... | collective-permute-start | bytes 393224 | tf_op jit(solution)/shard_map/ppermute | solution.py:20
  329.6 2.3 copy-start.3
  329.7 2.5 copy-start.8
  338.2 18.6 %copy-start.16 = (s32[1,256]{1,0:T(1,128)S(1)}, s32[1,256]{1,0:T(1,128)}, u32[]{:S(2)}) copy-start(s32[1,256]{1,0:T(1,128)} %param.11) | copy-start | bytes 3076
  338.2 18.6 %copy-start.17 = (f32[1,256]{1,0:T(1,128)S(1)}, f32[1,256]{1,0:T(1,128)}, u32[]{:S(2)}) copy-start(f32[1,256]{1,0:T(1,128)} %param.10) | copy-start | bytes 3076
  338.2 92.9 %copy-start.15 = (f32[1,256,128]{2,1,0:T(8,128)S(1)}, f32[1,256,128]{2,1,0:T(8,128)}, u32[]{:S(2)}) copy-start(f32[1,256,128]{2,1,0:T(8,128)} %param.13) | copy-start | bytes 393220
  338.6 6.4 %collective-permute-start.8 = (f32[1,256]{1,0:T(1,128)S(1)}, f32[1,256]{1,0:T(1,128)S(1)}, u32[]{:S(2)}, u32[]{:S(2)}) collective-permute-start(f32[1,256]{1,0:T(1,128)S(1)} %div.18), channel_id=1, source_target_pairs={{0,128},{8,136},{16,144},{24,152},{32,160},{40,168},{48,176},{56,1... | collective-permute-start | bytes 3080 | tf_op jit(solution)/shard_map/ppermute | solution.py:32
  (4 other events, 4.6 us)
Sparse Core Ops, SparseCore 0:
  16.5 239.7 all-reduce.10
where the time goes:
time: 439 us
  waiting for transfers between devices  242 us (55%)
  blocking collectives  83.8 us (19%)
  other arithmetic  57.7 us (13%)
  starting transfers between devices  25.5 us (6%)
  between operations  14.5 us (3%)
  local copies, waits for them, and re-layouts  12.7 us (3%)
    psum x1, waiting for transfers between devices, shards(): lax.psum((gram_local, proj_local), ('wide', 'slab'))  237 us
    psum x1, blocking collectives, shards(): lax.psum((gram_local, proj_local), ('wide', 'slab'))  73.7 us
    add x4, other arithmetic, march_forward(): centre + STEP_SIZE * (diffuse_subdomain.astype(jnp.float32) * spread - ca...  21.7 us
    ppermute x4, starting transfers between devices, padded(): lax.ppermute(tail, axis, [(i, (i + 1) % count) for i in range(ends)])  13.7 us
    another operation x3, other arithmetic, shards(): lower_factor = jnp.linalg.cholesky(gram_matrix)  13.2 us
    another operation x2, other arithmetic, shards(): lax.linalg.triangular_solve(lower_factor, half_solve, left_side=True, low...  11.9 us
    ppermute x4, starting transfers between devices, padded(): lax.ppermute(head, axis, [((i + 1) % count, i) for i in range(ends)])  10.9 us
    all_gather x1, blocking collectives, shards(): partner_all = lax.all_gather(partner_own, 'slab', axis=1, tiled=True)  10.1 us
  transfers between devices with their start and end apart: 10, of which 3 were waited for; matrix products, arithmetic and copies ran while one was open for 7% of the time, Pallas kernels for 0%

commit v1 on v0

--- a/solution.py
+++ b/solution.py
@@ -102,7 +102,12 @@
     face_means = face_means.reshape(1, rows_dev)
     top_bit = lax.axis_size("wide").bit_length() - 2
     partner_own = partner(face_means, "wide", top_bit)
-    partner_all = lax.all_gather(partner_own, "slab", axis=1, tiled=True)
+    ring = [partner_own]
+    for hop in range(7):
+        ring.append(lax.ppermute(ring[-1], "slab", [(dev, (dev + 1) % 8) for dev in range(8)]))
+    partner_all = jnp.roll(
+        jnp.concatenate(ring[::-1], axis=1), (lax.axis_index("slab") + 1) * ring[0].shape[1], axis=1
+    )
     tilde = jnp.take(partner_all[0], partner_facing_rows[0], axis=0)
     resid = tilde - interface_guess[0]
     proj_local = jnp.dot(

time: 439 us -> 426 us (0.970)
  starting transfers between devices: 25.5 us -> 42.4 us
  waiting for transfers between devices: 242 us -> 226 us
  blocking collectives: 83.8 us -> 75.6 us
    psum x1, waiting for transfers between devices: 237 us -> 217 us  [shards(): lax.psum((gram_local, proj_local), ('wide', 'slab'))]
    ppermute x0 -> x7, starting transfers between devices: none -> 10.4 us  [shards(): lax.ppermute(ring[-1], 'slab', [(dev, (dev + 1) % 8) for dev in range(8)])]
    all_gather x1 -> x0, blocking collectives: 10.1 us -> none  [shards(): partner_all = lax.all_gather(partner_own, 'slab', axis=1, tiled=True)]
    ppermute x1, starting transfers between devices: 0.88 us -> 6.3 us  [partner(): return lax.ppermute(value, axis, pairs)]
  transfers between devices with their start and end apart: 10 -> 17, of which waited for: 3 -> 11; matrix products, arithmetic and copies ran while one was open for 7% -> 8% of each run, Pallas kernels for 0% -> 0%
where the time goes in v1:
time: 426 us; the launch traced here: 425 us
  waiting for transfers between devices  226 us (53%)
  blocking collectives  75.6 us (18%)
  other arithmetic  53.9 us (13%)
  starting transfers between devices  42.4 us (10%)
  between operations  14.5 us (3%)
  local copies, waits for them, and re-layouts  10.4 us (2%)
    psum x1, waiting for transfers between devices, shards(): lax.psum((gram_local, proj_local), ('wide', 'slab'))  217 us
    psum x1, blocking collectives, shards(): lax.psum((gram_local, proj_local), ('wide', 'slab'))  75.6 us
    add x4, other arithmetic, march_forward(): centre + STEP_SIZE * (diffuse_subdomain.astype(jnp.float32) * spread - ca...  22.5 us
    ppermute x4, starting transfers between devices, padded(): lax.ppermute(tail, axis, [(i, (i + 1) % count) for i in range(ends)])  14.3 us
    another operation x3, other arithmetic, shards(): lower_factor = jnp.linalg.cholesky(gram_matrix)  12.4 us
    ppermute x4, starting transfers between devices, padded(): lax.ppermute(head, axis, [((i + 1) % count, i) for i in range(ends)])  11.4 us
    another operation x2, other arithmetic, shards(): lax.linalg.triangular_solve(lower_factor, half_solve, left_side=True, low...  10.5 us
    ppermute x7, starting transfers between devices, shards(): lax.ppermute(ring[-1], 'slab', [(dev, (dev + 1) % 8) for dev in range(8)])  10.4 us
  transfers between devices with their start and end apart: 17, of which 11 were waited for; matrix products, arithmetic and copies ran while one was open for 8% of the time, Pallas kernels for 0%

profile of v1, /device:TPU:1, one launch (start us, length us, event | category | flops | bytes accessed | tf_op | source)
XLA Modules:
  0.0 425.4 jit_solution(15224083714111179591)
XLA Ops:
  8.2 5.1 %collective-permute-start = (f32[1,32,1024]{2,1,0:T(8,128)S(1)}, f32[1,32,1024]{2,1,0:T(8,128)S(1)}, u32[]{:S(2)}, u32[]{:S(2)}) collective-permute-start(f32[1,32,1024]{2,1,0:T(8,128)S(1)} %get-tuple-element.16), channel_id=1, source_target_pairs={{1,0},{2,1},{3,2},{4,3},{5,4},{6,5},{7,6},{9,8},{10,9},{11,10},{12... | collective-permute-start | bytes 393224 | tf_op jit(solution)/shard_map/ppermute | solution.py:22
  13.4 1.9 collective-permute-start.1
  18.2 2.3 pad_maximum_fusion.3
  21.1 7.0 %fusion.2 = f32[16,32,1024]{2,1,0:T(8,128)S(1)} fusion(f32[16,32,1024]{2,1,0:T(8,128)} %bitcast.90, f32[18,34,1024]{2,1,0:T(8,128)S(1)} %pad_maximum_fusion.3, f32[1,32,1024]{2,1,0:T(8,128)S(1)} %collective-permute-done, f32[1,32,1024]{2,1,0:T(8,128)S(1)} %copy-done.8, f32[18,1,1024]{2,1,0:T(1,128)S(1)} %broadcast_in_dim.30, ...), kind=kLoop, calls=%fused_computation.35 | loop fusion | flops 18874368 | bytes 11231232 | tf_op jit(solution)/shard_map/add | solution.py:63
  28.1 2.4 collective-permute-start.2
  30.5 3.5 collective-permute-start.3
  36.7 5.4 %fusion.5 = f32[16,32,1024]{2,1,0:T(8,128)S(1)} fusion(f32[16,32,1024]{2,1,0:T(8,128)S(1)} %fusion.2, f32[18,34,1024]{2,1,0:T(8,128)S(1)} %pad_maximum_fusion.2, f32[1,32,1024]{2,1,0:T(8,128)S(1)} %collective-permute-done.2, f32[1,32,1024]{2,1,0:T(8,128)S(1)} %collective-permute-done.3, f32[18,1,1024]{2,1,0:T(1,128)S(1)} %broadcast_in_dim.30, ...), kind=kLoop, calls=%fused_computation.38 | loop fusion | flops 18874368 | bytes 11231232 | tf_op jit(solution)/shard_map/add | solution.py:63
  42.1 1.9 collective-permute-start.4
  44.0 4.4 %collective-permute-start.5 = (f32[1,32,1024]{2,1,0:T(8,128)S(1)}, f32[1,32,1024]{2,1,0:T(8,128)S(1)}, u32[]{:S(2)}, u32[]{:S(2)}) collective-permute-start(f32[1,32,1024]{2,1,0:T(8,128)S(1)} %get-tuple-element.11), channel_id=1, source_target_pairs={{0,1},{1,2},{2,3},{3,4},{4,5},{5,6},{6,7},{8,9},{9,10},{10,11},{11... | collective-permute-start | bytes 393224 | tf_op jit(solution)/shard_map/ppermute | solution.py:20
  51.0 5.4 %fusion.8 = f32[16,32,1024]{2,1,0:T(8,128)S(1)} fusion(f32[16,32,1024]{2,1,0:T(8,128)S(1)} %fusion.5, f32[18,34,1024]{2,1,0:T(8,128)S(1)} %pad_maximum_fusion.1, f32[1,32,1024]{2,1,0:T(8,128)S(1)} %collective-permute-done.4, f32[1,32,1024]{2,1,0:T(8,128)S(1)} %collective-permute-done.5, f32[18,1,1024]{2,1,0:T(1,128)S(1)} %broadcast_in_dim.30, ...), kind=kLoop, calls=%fused_computation.41 | loop fusion | flops 18874368 | bytes 11231232 | tf_op jit(solution)/shard_map/add | solution.py:63
  58.5 1.9 collective-permute-start.6
  60.4 4.5 %collective-permute-start.7 = (f32[1,32,1024]{2,1,0:T(8,128)}, f32[1,32,1024]{2,1,0:T(8,128)}, u32[]{:S(2)}, u32[]{:S(2)}) collective-permute-start(f32[1,32,1024]{2,1,0:T(8,128)} %get-tuple-element.9), channel_id=1, source_target_pairs={{0,1},{1,2},{2,3},{3,4},{4,5},{5,6},{6,7},{8,9},{9,10},{10,11},{11... | collective-permute-start | bytes 393224 | tf_op jit(solution)/shard_map/ppermute | solution.py:20
  67.0 2.1 pad_maximum_fusion
  69.1 4.7 %fusion.11 = f32[16,32,1024]{2,1,0:T(8,128)S(1)} fusion(f32[16,32,1024]{2,1,0:T(8,128)S(1)} %copy-done.3, f32[18,34,1024]{2,1,0:T(8,128)S(1)} %pad_maximum_fusion, f32[1,32,1024]{2,1,0:T(8,128)S(1)} %collective-permute-done.6, f32[1,32,1024]{2,1,0:T(8,128)} %collective-permute-done.7, f32[18,1,1024]{2,1,0:T(1,128)S(1)} %broadcast_in_dim.30, ...), kind=kLoop, calls=%fused_computation.44 | loop fusion | flops 18874368 | bytes 11231232 | tf_op jit(solution)/shard_map/add | solution.py:63
  75.6 6.3 %collective-permute-start.8 = (f32[1,256]{1,0:T(1,128)S(1)}, f32[1,256]{1,0:T(1,128)S(1)}, u32[]{:S(2)}, u32[]{:S(2)}) collective-permute-start(f32[1,256]{1,0:T(1,128)S(1)} %div.18), channel_id=1, source_target_pairs={{0,128},{8,136},{16,144},{24,152},{32,160},{40,168},{48,176},{56,1... | collective-permute-start | bytes 3080 | tf_op jit(solution)/shard_map/ppermute | solution.py:32
  82.8 3.3 collective-permute-start.9
  86.9 2.3 collective-permute-start.10
  89.2 216.9 %all-reduce.11.cloned.1.call-done = f32[128,128]{0,1:T(8,128)} async-done(((f32[128,128]{0,1:T(8,128)}), f32[128,128]{0,1:T(8,128)}) %all-reduce.11.cloned.1.call-update) | async-done | bytes 65552 | tf_op jit(solution)/shard_map/psum | solution.py:116
  308.5 11.7 %cholesky.16 = f32[128,128]{1,0:T(8,128)S(1)} custom-call(f32[128,128]{1,0:T(8,128)S(1)} %fusion.45), custom_call_target="Cholesky" | custom-call | tf_op jit(solution)/shard_map/jit(cholesky)/cholesky | solution.py:117
  321.4 2.2 collective-permute-start.13
  324.9 1.6 collective-permute-start.14
  327.2 9.8 %custom-call.10 = f32[1,128,128]{1,2,0:T(8,128)S(1)} custom-call(f32[1,128,128]{2,1,0:T(8,128)S(1)} %fusion.41), custom_call_target="InvertDiagBlocksLowerTriangular" | custom-call | tf_op jit(solution)/shard_map/triangular_solve | solution.py:121
  339.8 1.7 gather_fusion
  341.8 75.6 %psum.15 = f32[128]{0:T(128)S(1)} all-reduce(f32[128]{0:T(128)S(1)} %convolution_bitcast_fusion.2), channel_id=1, replica_groups=mesh['wide'=32,'slab'=8] {'wide','slab'}, use_global_device_ids=true, to_apply=%region_4.5 | all-reduce | flops 128 | bytes 1024 | tf_op jit(solution)/shard_map/psum | solution.py:116
  (96 shorter events, 26.9 us)
Async XLA Ops:
  7.2 57.8 %copy-start = (f32[1,256,128]{2,1,0:T(8,128)S(1)}, f32[1,256,128]{2,1,0:T(8,128)}, u32[]{:S(2)}) copy-start(f32[1,256,128]{2,1,0:T(8,128)} %param.12) | copy-start | bytes 393220
  7.2 298.9 %all-reduce.11.cloned.1.call-start = ((), (), s32[]{:S(2)}) async-start(), calls=%async_computation | async-start | bytes 131072 | tf_op jit(solution)/shard_map/psum | solution.py:116
  8.2 9.3 %collective-permute-start = (f32[1,32,1024]{2,1,0:T(8,128)S(1)}, f32[1,32,1024]{2,1,0:T(8,128)S(1)}, u32[]{:S(2)}, u32[]{:S(2)}) collective-permute-start(f32[1,32,1024]{2,1,0:T(8,128)S(1)} %get-tuple-element.16), channel_id=1, source_target_pairs={{1,0},{2,1},{3,2},{4,3},{5,4},{6,5},{7,6},{9,8},{10,9},{11,10},{12... | collective-permute-start | bytes 393224 | tf_op jit(solution)/shard_map/ppermute | solution.py:22
  13.4 4.2 collective-permute-start.1
  18.2 2.8 copy-start.8
  28.1 6.7 %collective-permute-start.2 = (f32[1,32,1024]{2,1,0:T(8,128)S(1)}, f32[1,32,1024]{2,1,0:T(8,128)S(1)}, u32[]{:S(2)}, u32[]{:S(2)}) collective-permute-start(f32[1,32,1024]{2,1,0:T(8,128)S(1)} %get-tuple-element.14), channel_id=1, source_target_pairs={{1,0},{2,1},{3,2},{4,3},{5,4},{6,5},{7,6},{9,8},{10,9},{11,10},{12... | collective-permute-start | bytes 393224 | tf_op jit(solution)/shard_map/ppermute | solution.py:22
  30.5 5.5 %collective-permute-start.3 = (f32[1,32,1024]{2,1,0:T(8,128)S(1)}, f32[1,32,1024]{2,1,0:T(8,128)S(1)}, u32[]{:S(2)}, u32[]{:S(2)}) collective-permute-start(f32[1,32,1024]{2,1,0:T(8,128)S(1)} %get-tuple-element.13), channel_id=1, source_target_pairs={{0,1},{1,2},{2,3},{3,4},{4,5},{5,6},{6,7},{8,9},{9,10},{10,11},{11... | collective-permute-start | bytes 393224 | tf_op jit(solution)/shard_map/ppermute | solution.py:20
  42.1 7.0 %collective-permute-start.4 = (f32[1,32,1024]{2,1,0:T(8,128)S(1)}, f32[1,32,1024]{2,1,0:T(8,128)S(1)}, u32[]{:S(2)}, u32[]{:S(2)}) collective-permute-start(f32[1,32,1024]{2,1,0:T(8,128)S(1)} %get-tuple-element.12), channel_id=1, source_target_pairs={{1,0},{2,1},{3,2},{4,3},{5,4},{6,5},{7,6},{9,8},{10,9},{11,10},{12... | collective-permute-start | bytes 393224 | tf_op jit(solution)/shard_map/ppermute | solution.py:22
  44.0 6.3 %collective-permute-start.5 = (f32[1,32,1024]{2,1,0:T(8,128)S(1)}, f32[1,32,1024]{2,1,0:T(8,128)S(1)}, u32[]{:S(2)}, u32[]{:S(2)}) collective-permute-start(f32[1,32,1024]{2,1,0:T(8,128)S(1)} %get-tuple-element.11), channel_id=1, source_target_pairs={{0,1},{1,2},{2,3},{3,4},{4,5},{5,6},{6,7},{8,9},{9,10},{10,11},{11... | collective-permute-start | bytes 393224 | tf_op jit(solution)/shard_map/ppermute | solution.py:20
  58.5 7.5 %collective-permute-start.6 = (f32[1,32,1024]{2,1,0:T(8,128)}, f32[1,32,1024]{2,1,0:T(8,128)S(1)}, u32[]{:S(2)}, u32[]{:S(2)}) collective-permute-start(f32[1,32,1024]{2,1,0:T(8,128)} %get-tuple-element.10), channel_id=1, source_target_pairs={{1,0},{2,1},{3,2},{4,3},{5,4},{6,5},{7,6},{9,8},{10,9},{11,10},{12... | collective-permute-start | bytes 393224 | tf_op jit(solution)/shard_map/ppermute | solution.py:22
  60.4 6.6 %collective-permute-start.7 = (f32[1,32,1024]{2,1,0:T(8,128)}, f32[1,32,1024]{2,1,0:T(8,128)}, u32[]{:S(2)}, u32[]{:S(2)}) collective-permute-start(f32[1,32,1024]{2,1,0:T(8,128)} %get-tuple-element.9), channel_id=1, source_target_pairs={{0,1},{1,2},{2,3},{3,4},{4,5},{5,6},{6,7},{8,9},{9,10},{10,11},{11... | collective-permute-start | bytes 393224 | tf_op jit(solution)/shard_map/ppermute | solution.py:20
  66.0 3.1 copy-start.3
  66.0 3.1 copy-start.5
  69.1 12.8 %copy-start.10 = (s32[1,256]{1,0:T(1,128)S(1)}, s32[1,256]{1,0:T(1,128)}, u32[]{:S(2)}) copy-start(s32[1,256]{1,0:T(1,128)} %param.11) | copy-start | bytes 3076
  75.1 266.4 %copy-start.11 = (f32[1,256]{1,0:T(1,128)S(1)}, f32[1,256]{1,0:T(1,128)}, u32[]{:S(2)}) copy-start(f32[1,256]{1,0:T(1,128)} %param.10) | copy-start | bytes 3076
  75.1 342.6 %copy-start.9 = (f32[1,256,128]{2,1,0:T(8,128)S(1)}, f32[1,256,128]{2,1,0:T(8,128)}, u32[]{:S(2)}) copy-start(f32[1,256,128]{2,1,0:T(8,128)} %param.13) | copy-start | bytes 393220
  75.6 7.3 %collective-permute-start.8 = (f32[1,256]{1,0:T(1,128)S(1)}, f32[1,256]{1,0:T(1,128)S(1)}, u32[]{:S(2)}, u32[]{:S(2)}) collective-permute-start(f32[1,256]{1,0:T(1,128)S(1)} %div.18), channel_id=1, source_target_pairs={{0,128},{8,136},{16,144},{24,152},{32,160},{40,168},{48,176},{56,1... | collective-permute-start | bytes 3080 | tf_op jit(solution)/shard_map/ppermute | solution.py:32
  82.8 4.0 collective-permute-start.9
  86.9 220.1 %collective-permute-start.10 = (f32[1,256]{1,0:T(1,128)S(1)}, f32[1,256]{1,0:T(1,128)S(1)}, u32[]{:S(2)}, u32[]{:S(2)}) collective-permute-start(f32[1,256]{1,0:T(1,128)S(1)} %collective-permute-done.9), channel_id=1, source_target_pairs={{0,1},{1,2},{2,3},{3,4},{4,5},{5,6},{6,7},{7,0},{8,9},{9,10},{10,1... | collective-permute-start | bytes 3080 | tf_op jit(solution)/shard_map/ppermute | solution.py:107
  307.0 13.2 %collective-permute-start.11 = (f32[1,256]{1,0:T(1,128)S(1)}, f32[1,256]{1,0:T(1,128)S(1)}, u32[]{:S(2)}, u32[]{:S(2)}) collective-permute-start(f32[1,256]{1,0:T(1,128)S(1)} %collective-permute-done.10), channel_id=1, source_target_pairs={{0,1},{1,2},{2,3},{3,4},{4,5},{5,6},{6,7},{7,0},{8,9},{9,10},{10,1... | collective-permute-start | bytes 3080 | tf_op jit(solution)/shard_map/ppermute | solution.py:107
  320.2 1.1 collective-permute-start.12
  321.4 3.6 collective-permute-start.13
  324.9 12.1 %collective-permute-start.14 = (f32[1,256]{1,0:T(1,128)S(1)}, f32[1,256]{1,0:T(1,128)S(1)}, u32[]{:S(2)}, u32[]{:S(2)}) collective-permute-start(f32[1,256]{1,0:T(1,128)S(1)} %collective-permute-done.13), channel_id=1, source_target_pairs={{0,1},{1,2},{2,3},{3,4},{4,5},{5,6},{6,7},{7,0},{8,9},{9,10},{10,1... | collective-permute-start | bytes 3080 | tf_op jit(solution)/shard_map/ppermute | solution.py:107
  337.0 2.6 collective-permute-start.15
  (5 other events, 8.7 us)
Sparse Core Ops, SparseCore 0:
  66.1 239.9 all-reduce.10
